TPU v7x, 32 devices: a whole 2x2x4 slice. The times are simulated.
32 devices in a mesh: rep: 4 (over y, core), shard: 8 (over z, x).
Axes of the slice: x: 2, y: 2, z: 4, core: 2. Of those that a mesh axis runs over, the one named last changes fastest.
Arguments:
- weights: bfloat16 [4, 4096, 5120], P('rep', 'shard'), may hold values from -12 to 12
- warm_start: bfloat16 [4, 2, 16, 5120], P('rep'), may hold values from -4 to 4, as said below
Outputs:
- corrected: bfloat16 [4, 4096, 5120], P('rep', 'shard')
- factors: float32 [4, 2, 16, 5120], P('rep')
Inputs may be any that keep to these rules, and one draw needn't show every extreme that they name: `warm_start`: replicas whose indices differ only in bit 0 hold equal start vectors for matching 0, and replicas whose indices differ by 2 hold equal start vectors for matching 1.
All inputs are finite; a program needn't handle non-finite values.
Results may differ from a plain program's by a relative error of at most 0.0049.
Values sent between devices are 32-bit elements; how exact they have to be, the bound alone decides.
A program may use at most 64 MiB of HBM per device.

v0:
```python
import jax
import jax.numpy as jnp
from jax import lax
from jax.sharding import PartitionSpec as P

STEPS = 2


def partner(value, axis, stride):
    return lax.ppermute(value, axis, [(i, i ^ 1 << stride) for i in range(lax.axis_size(axis))])


def shards(weights, warm_start):
    current = weights[0]
    replica = lax.axis_index("rep")
    half_rep = lax.axis_size("rep") // 2
    top_bit = lax.axis_size("rep").bit_length() - 2
    factor_list = []
    for matching in range(STEPS):
        if matching == 0:
            bit_number = 0
            parity = 1.0 - 2.0 * (replica % 2).astype(jnp.float32)
        else:
            bit_number = top_bit
            parity = 1.0 - 2.0 * (replica // half_rep).astype(jnp.float32)
        starts = warm_start[0, matching]
        sketch = lax.dot_general(
            starts, current, (((1,), (1,)), ((), ())), preferred_element_type=jnp.float32
        )
        sketch_other = partner(sketch, "rep", bit_number)
        differ = parity * (sketch - sketch_other)
        gram_local = lax.dot_general(
            differ, differ, (((1,), (1,)), ((), ())), precision=lax.Precision.HIGHEST
        )
        gram_sum = lax.psum(gram_local, "shard")
        triangle = jnp.linalg.cholesky(gram_sum)
        basis_rows = lax.linalg.triangular_solve(triangle, differ, left_side=True, lower=True)
        signed = parity * jnp.dot(
            basis_rows.astype(jnp.bfloat16), current, preferred_element_type=jnp.float32
        )
        summed = lax.psum(signed, "shard")
        factors = summed + partner(summed, "rep", bit_number)
        change = lax.dot_general(
            basis_rows, factors, (((0,), (0,)), ((), ())), precision=lax.Precision.HIGHEST
        )
        current = (current.astype(jnp.float32) - 0.5 * parity * change).astype(jnp.bfloat16)
        factor_list.append(factors)
    return (current[None], jnp.stack(factor_list)[None])


def solution(mesh):
    placed = (P("rep", "shard", None), P("rep", None, None, None))
    return jax.shard_map(
        shards,
        mesh=mesh,
        in_specs=placed,
        out_specs=(P("rep", "shard", None), P("rep", None, None, None)),
        check_vma=False,
    )
```

profile of v0, /device:TPU:0, one launch (start us, length us, event | category | flops | bytes accessed | tf_op | source)
XLA Modules:
  0.0 259.3 jit_solution(16875092373942699540)
XLA Ops:
  7.2 4.0 %fusion.2 = f32[16,512]{1,0:T(8,128)S(1)} fusion(bf16[1,512,5120]{2,1,0:T(8,128)(2,1)} %param.5, bf16[1,2,16,5120]{3,2,1,0:T(8,128)(2,1)} %param.6), kind=kOutput, calls=%fused_computation.6 | convolution fusion | flops 83886080 | bytes 5439488 | tf_op jit(solution)/shard_map/dot_general | solution.py:27
  11.2 0.5 collective-permute-start
  11.7 0.9 collective-permute-done
  12.6 0.1 fusion.13
  12.7 23.2 %psum.28 = f32[16,16]{0,1:T(8,128)S(1)} all-reduce(f32[16,16]{0,1:T(8,128)S(1)} %fusion.13), channel_id=1, replica_groups=mesh['rep'=4,'shard'=8] {'shard'}, use_global_device_ids=true, to_apply=%region_0.1 | all-reduce | flops 256 | bytes 2048 | tf_op jit(solution)/shard_map/psum | solution.py:35
  36.1 1.5 cholesky.44
  37.6 0.6 compare_reduce_fusion.1
  38.2 0.6 fusion.16
  38.9 1.2 custom-call.6
  40.1 0.2 fusion.12
  40.3 4.0 %convolution_multiply_fusion.1 = f32[16,5120]{1,0:T(8,128)} fusion(bf16[1,512,5120]{2,1,0:T(8,128)(2,1)} %param.5, f32[]{:T(128)S(6)} %sub.22, f32[16,512]{1,0:T(8,128)S(1)} %fusion.12), kind=kOutput, calls=%fused_computation.4 | convolution fusion | flops 83976192 | bytes 5603332 | tf_op jit(solution)/shard_map/dot_general | solution.py:38
  44.4 68.8 %all-reduce.3.cloned.1.call-done = f32[16,5120]{1,0:T(8,128)} async-done(((f32[16,5120]{1,0:T(8,128)}), f32[16,5120]{1,0:T(8,128)}) %all-reduce.3.cloned.1.call-update) | async-done | bytes 327696 | tf_op jit(solution)/shard_map/psum | solution.py:41
  113.2 1.8 collective-permute-done.1
  115.0 10.8 %subtract_convert_fusion.1 = bf16[512,5120]{1,0:T(8,128)(2,1)S(1)} fusion(f32[16,512]{1,0:T(8,128)S(1)} %fusion.12, bf16[1,512,5120]{2,1,0:T(8,128)(2,1)} %param.5, f32[]{:T(128)S(6)} %mul.49, f32[16,5120]{1,0:T(8,128)} %all-reduce.3.cloned.1.call-done, f32[16,5120]{1,0:T(8,128)S(1)} %collective-permute-done.1), kind=kOutput, calls=%fused_computation.1 | convolution fusion | flops 513884160 | bytes 11173892 | tf_op jit(solution)/shard_map/dot_general | solution.py:43
  125.9 2.3 copy-done
  128.2 1.5 convolution_bitcast_fusion
  129.7 1.5 collective-permute-start.2
  131.2 2.4 collective-permute-done.2
  133.6 0.1 fusion.15
  133.8 19.9 %psum.30 = f32[16,16]{0,1:T(8,128)S(1)} all-reduce(f32[16,16]{0,1:T(8,128)S(1)} %fusion.15), channel_id=1, replica_groups=mesh['rep'=4,'shard'=8] {'shard'}, use_global_device_ids=true, to_apply=%region_4.7 | all-reduce | flops 256 | bytes 2048 | tf_op jit(solution)/shard_map/psum | solution.py:35
  153.7 1.5 cholesky.55
  155.2 0.6 compare_reduce_fusion
  155.9 0.6 fusion.17
  156.5 1.2 custom-call.7
  157.8 0.2 fusion.14
  158.0 4.0 %convolution_multiply_fusion = f32[16,5120]{1,0:T(8,128)} fusion(bf16[512,5120]{1,0:T(8,128)(2,1)} %copy-done, f32[]{:T(128)S(6)} %sub.26, f32[16,512]{1,0:T(8,128)S(1)} %fusion.14), kind=kOutput, calls=%fused_computation.3 | convolution fusion | flops 83976192 | bytes 5603332 | tf_op jit(solution)/shard_map/dot_general | solution.py:38
  162.0 68.8 %all-reduce.5.cloned.1.call-done = f32[16,5120]{1,0:T(8,128)} async-done(((f32[16,5120]{1,0:T(8,128)}), f32[16,5120]{1,0:T(8,128)}) %all-reduce.5.cloned.1.call-update) | async-done | bytes 327696 | tf_op jit(solution)/shard_map/psum | solution.py:41
  230.8 1.5 collective-permute-start.3
  232.3 6.3 %collective-permute-done.3 = f32[16,5120]{1,0:T(8,128)S(1)} collective-permute-done((f32[16,5120]{1,0:T(8,128)}, f32[16,5120]{1,0:T(8,128)S(1)}, u32[]{:S(2)}, u32[]{:S(2)}) %collective-permute-start.3) | collective-permute-done | bytes 327712 | tf_op jit(solution)/shard_map/ppermute | solution.py:10
  238.6 1.0 add_bitcast_fusion
  239.6 0.9 maximum_bitcast_fusion
  240.5 11.9 %fusion = bf16[1,512,5120]{2,1,0:T(8,128)(2,1)} fusion(f32[16,512]{1,0:T(8,128)S(1)} %fusion.14, bf16[512,5120]{1,0:T(8,128)(2,1)} %copy-done, f32[]{:T(128)S(6)} %mul.57, f32[16,5120]{1,0:T(8,128)} %all-reduce.5.cloned.1.call-done, f32[16,5120]{1,0:T(8,128)S(1)} %collective-permute-done.3), kind=kOutput, calls=%fused_computation.2 | convolution fusion | flops 513884160 | bytes 11173892 | tf_op jit(solution)/shard_map/dot_general | solution.py:43
  (17 shorter events, 0.4 us)
Async XLA Ops:
  7.2 106.0 %all-reduce.3.cloned.1.call-start = ((), (), s32[]{:S(2)}) async-start(), calls=%async_computation | async-start | bytes 655360 | tf_op jit(solution)/shard_map/psum | solution.py:41
  11.2 1.4 collective-permute-start
  44.4 186.4 %all-reduce.5.cloned.1.call-start = ((), (), s32[]{:S(2)}) async-start(), calls=%async_computation.1 | async-start | bytes 655360 | tf_op jit(solution)/shard_map/psum | solution.py:41
  113.2 1.8 collective-permute-start.1
  113.2 15.0 %copy-start.2 = (bf16[1,2,16,5120]{3,2,1,0:T(8,128)(2,1)S(1)}, bf16[1,2,16,5120]{3,2,1,0:T(8,128)(2,1)}, u32[]{:S(2)}) copy-start(bf16[1,2,16,5120]{3,2,1,0:T(8,128)(2,1)} %param.6) | copy-start | bytes 983044
  125.9 2.4 copy-start
  128.2 104.0 %copy-start.1 = (f32[16,5120]{1,0:T(8,128)S(1)}, f32[16,5120]{1,0:T(8,128)}, u32[]{:S(2)}) copy-start(f32[16,5120]{1,0:T(8,128)} %all-reduce.3.cloned.1.call-done) | copy-start | bytes 983044
  129.7 3.9 %collective-permute-start.2 = (f32[16,512]{1,0:T(8,128)S(1)}, f32[16,512]{1,0:T(8,128)S(1)}, u32[]{:S(2)}, u32[]{:S(2)}) collective-permute-start(f32[16,512]{1,0:T(8,128)S(1)} %convolution_bitcast_fusion), channel_id=1, source_target_pairs={{0,16},{8,24},{16,0},{24,8},{1,17},{9,25},{17,1},{25,9},{2,18},{10... | collective-permute-start | bytes 98312 | tf_op jit(solution)/shard_map/ppermute | solution.py:10
  230.8 7.8 %collective-permute-start.3 = (f32[16,5120]{1,0:T(8,128)}, f32[16,5120]{1,0:T(8,128)S(1)}, u32[]{:S(2)}, u32[]{:S(2)}) collective-permute-start(f32[16,5120]{1,0:T(8,128)} %all-reduce.5.cloned.1.call-done), channel_id=1, source_target_pairs={{0,16},{8,24},{16,0},{24,8},{1,17},{9,25},{17,1},{25,9},{2,18},{10... | collective-permute-start | bytes 983048 | tf_op jit(solution)/shard_map/ppermute | solution.py:10
Sparse Core Ops, SparseCore 0:
  44.5 68.6 all-reduce.2
  162.2 68.5 all-reduce.4
where the time goes:
time: 260 us; the launch traced here: 259 us
  waiting for transfers between devices  149 us (57%)
  blocking collectives  43.1 us (17%)
  matrix products  37 us (14%)
  between operations  14.1 us (5%)
  other arithmetic  9.97 us (4%)
  starting transfers between devices  3.53 us (1%)
    psum x2, waiting for transfers between devices, shards(): summed = lax.psum(signed, 'shard')  138 us
    psum x2, blocking collectives, shards(): gram_sum = lax.psum(gram_local, 'shard')  43.1 us
    dot_general x2, matrix products, shards(): lax.dot_general(basis_rows, factors, (((0,), (0,)), ((), ())), precision=...  22.7 us
    ppermute x4, waiting for transfers between devices, partner(): lax.ppermute(value, axis, [(i, i ^ 1 << stride) for i in range(lax.axis_s...  11.5 us
    dot_general x2, matrix products, shards(): jnp.dot(basis_rows.astype(jnp.bfloat16), current, preferred_element_type=...  8.02 us
    dot_general x2, matrix products, shards(): lax.dot_general(starts, current, (((1,), (1,)), ((), ())), preferred_elem...  5.49 us
  transfers between devices with their start and end apart: 6, of which 6 were waited for; matrix products, arithmetic and copies ran while one was open for 0% of the time, Pallas kernels for 0%

commit v1 on v0

--- a/solution.py
+++ b/solution.py
@@ -32,7 +32,8 @@
         gram_local = lax.dot_general(
             differ, differ, (((1,), (1,)), ((), ())), precision=lax.Precision.HIGHEST
         )
-        gram_sum = lax.psum(gram_local, "shard")
+        terms = lax.all_gather(gram_local, "shard")
+        gram_sum = jnp.sum(terms, axis=0)
         triangle = jnp.linalg.cholesky(gram_sum)
         basis_rows = lax.linalg.triangular_solve(triangle, differ, left_side=True, lower=True)
         signed = parity * jnp.dot(

time: 260 us -> 285 us (1.096)
  blocking collectives: 43.1 us -> 62.8 us
  waiting for transfers between devices: 149 us -> 155 us
    all_gather x0 -> x2, blocking collectives: none -> 62.8 us  [shards(): terms = lax.all_gather(gram_local, 'shard')]
    psum x2 -> x0, blocking collectives: 43.1 us -> none  [shards(): gram_sum = lax.psum(gram_local, 'shard')]
    psum x2, waiting for transfers between devices: 138 us -> 143 us  [shards(): summed = lax.psum(signed, 'shard')]
where the time goes in v1:
time: 285 us; the launch traced here: 284 us
  waiting for transfers between devices  155 us (54%)
  blocking collectives  62.8 us (22%)
  matrix products  37 us (13%)
  between operations  14.1 us (5%)
  other arithmetic  10 us (4%)
  starting transfers between devices  3.54 us (1%)
    psum x2, waiting for transfers between devices, shards(): summed = lax.psum(signed, 'shard')  143 us
    all_gather x2, blocking collectives, shards(): terms = lax.all_gather(gram_local, 'shard')  62.8 us
    dot_general x2, matrix products, shards(): lax.dot_general(basis_rows, factors, (((0,), (0,)), ((), ())), precision=...  22.7 us
    ppermute x4, waiting for transfers between devices, partner(): lax.ppermute(value, axis, [(i, i ^ 1 << stride) for i in range(lax.axis_s...  11.5 us
    dot_general x2, matrix products, shards(): jnp.dot(basis_rows.astype(jnp.bfloat16), current, preferred_element_type=...  8.02 us
  transfers between devices with their start and end apart: 6, of which 6 were waited for; matrix products, arithmetic and copies ran while one was open for 0% of the time, Pallas kernels for 0%

profile of v1, /device:TPU:0, one launch (start us, length us, event | category | flops | bytes accessed | tf_op | source)
XLA Modules:
  0.0 284.4 jit_solution(141980312301753384)
XLA Ops:
  7.2 4.0 %fusion.2 = f32[16,512]{1,0:T(8,128)S(1)} fusion(bf16[1,512,5120]{2,1,0:T(8,128)(2,1)} %param.5, bf16[1,2,16,5120]{3,2,1,0:T(8,128)(2,1)} %param.6), kind=kOutput, calls=%fused_computation.6 | convolution fusion | flops 83886080 | bytes 5439488 | tf_op jit(solution)/shard_map/dot_general | solution.py:27
  11.2 0.5 collective-permute-start
  11.7 0.9 collective-permute-done
  12.6 0.1 fusion.13
  12.7 32.2 %all-gather = f32[128,16]{1,0:T(8,128)S(1)} all-gather(f32[16,16]{1,0:T(8,128)S(1)} %fusion.13), channel_id=2, replica_groups=mesh['rep'=4,'shard'=8] {'shard'}, dimensions={0}, use_global_device_ids=true | all-gather | bytes 9216 | tf_op jit(solution)/shard_map/all_gather | solution.py:35
  45.1 1.4 cholesky.44
  46.6 0.6 compare_reduce_fusion.1
  47.2 0.6 fusion.16
  47.9 1.2 custom-call.6
  49.1 0.2 fusion.12
  49.3 4.0 %convolution_multiply_fusion.1 = f32[16,5120]{1,0:T(8,128)} fusion(bf16[1,512,5120]{2,1,0:T(8,128)(2,1)} %param.5, f32[]{:T(128)S(6)} %sub.22, f32[16,512]{1,0:T(8,128)S(1)} %fusion.12), kind=kOutput, calls=%fused_computation.4 | convolution fusion | flops 83976192 | bytes 5603332 | tf_op jit(solution)/shard_map/dot_general | solution.py:39
  53.4 72.4 %all-reduce.3.cloned.1.call-done = f32[16,5120]{1,0:T(8,128)} async-done(((f32[16,5120]{1,0:T(8,128)}), f32[16,5120]{1,0:T(8,128)}) %all-reduce.3.cloned.1.call-update) | async-done | bytes 327696 | tf_op jit(solution)/shard_map/psum | solution.py:42
  125.8 1.8 collective-permute-done.1
  127.6 10.8 %subtract_convert_fusion.1 = bf16[512,5120]{1,0:T(8,128)(2,1)S(1)} fusion(f32[16,512]{1,0:T(8,128)S(1)} %fusion.12, bf16[1,512,5120]{2,1,0:T(8,128)(2,1)} %param.5, f32[]{:T(128)S(6)} %mul.49, f32[16,5120]{1,0:T(8,128)} %all-reduce.3.cloned.1.call-done, f32[16,5120]{1,0:T(8,128)S(1)} %collective-permute-done.1), kind=kOutput, calls=%fused_computation.1 | convolution fusion | flops 513884160 | bytes 11173892 | tf_op jit(solution)/shard_map/dot_general | solution.py:44
  138.5 2.3 copy-done
  140.8 1.5 convolution_bitcast_fusion
  142.3 1.5 collective-permute-start.2
  143.8 2.4 collective-permute-done.2
  146.2 0.1 fusion.15
  146.3 30.6 %all-gather.1 = f32[128,16]{1,0:T(8,128)S(1)} all-gather(f32[16,16]{1,0:T(8,128)S(1)} %fusion.15), channel_id=3, replica_groups=mesh['rep'=4,'shard'=8] {'shard'}, dimensions={0}, use_global_device_ids=true | all-gather | bytes 9216 | tf_op jit(solution)/shard_map/all_gather | solution.py:35
  177.0 1.5 cholesky.55
  178.5 0.6 compare_reduce_fusion
  179.1 0.6 fusion.17
  179.8 1.2 custom-call.7
  181.0 0.2 fusion.14
  181.3 4.0 %convolution_multiply_fusion = f32[16,5120]{1,0:T(8,128)} fusion(bf16[512,5120]{1,0:T(8,128)(2,1)} %copy-done, f32[]{:T(128)S(6)} %sub.26, f32[16,512]{1,0:T(8,128)S(1)} %fusion.14), kind=kOutput, calls=%fused_computation.3 | convolution fusion | flops 83976192 | bytes 5603332 | tf_op jit(solution)/shard_map/dot_general | solution.py:39
  185.3 70.7 %all-reduce.5.cloned.1.call-done = f32[16,5120]{1,0:T(8,128)} async-done(((f32[16,5120]{1,0:T(8,128)}), f32[16,5120]{1,0:T(8,128)}) %all-reduce.5.cloned.1.call-update) | async-done | bytes 327696 | tf_op jit(solution)/shard_map/psum | solution.py:42
  256.0 1.5 collective-permute-start.3
  257.5 6.3 %collective-permute-done.3 = f32[16,5120]{1,0:T(8,128)S(1)} collective-permute-done((f32[16,5120]{1,0:T(8,128)}, f32[16,5120]{1,0:T(8,128)S(1)}, u32[]{:S(2)}, u32[]{:S(2)}) %collective-permute-start.3) | collective-permute-done | bytes 327712 | tf_op jit(solution)/shard_map/ppermute | solution.py:10
  263.8 1.0 add_bitcast_fusion
  264.8 0.9 maximum_bitcast_fusion
  265.7 11.9 %fusion = bf16[1,512,5120]{2,1,0:T(8,128)(2,1)} fusion(f32[16,512]{1,0:T(8,128)S(1)} %fusion.14, bf16[512,5120]{1,0:T(8,128)(2,1)} %copy-done, f32[]{:T(128)S(6)} %mul.57, f32[16,5120]{1,0:T(8,128)} %all-reduce.5.cloned.1.call-done, f32[16,5120]{1,0:T(8,128)S(1)} %collective-permute-done.3), kind=kOutput, calls=%fused_computation.2 | convolution fusion | flops 513884160 | bytes 11173892 | tf_op jit(solution)/shard_map/dot_general | solution.py:44
  (19 shorter events, 0.4 us)
Async XLA Ops:
  7.2 118.6 %all-reduce.3.cloned.1.call-start = ((), (), s32[]{:S(2)}) async-start(), calls=%async_computation | async-start | bytes 655360 | tf_op jit(solution)/shard_map/psum | solution.py:42
  11.2 1.4 collective-permute-start
  53.4 202.6 %all-reduce.5.cloned.1.call-start = ((), (), s32[]{:S(2)}) async-start(), calls=%async_computation.1 | async-start | bytes 655360 | tf_op jit(solution)/shard_map/psum | solution.py:42
  125.8 1.8 collective-permute-start.1
  125.8 15.0 %copy-start.2 = (bf16[1,2,16,5120]{3,2,1,0:T(8,128)(2,1)S(1)}, bf16[1,2,16,5120]{3,2,1,0:T(8,128)(2,1)}, u32[]{:S(2)}) copy-start(bf16[1,2,16,5120]{3,2,1,0:T(8,128)(2,1)} %param.6) | copy-start | bytes 983044
  138.5 2.4 copy-start
  140.8 116.6 %copy-start.1 = (f32[16,5120]{1,0:T(8,128)S(1)}, f32[16,5120]{1,0:T(8,128)}, u32[]{:S(2)}) copy-start(f32[16,5120]{1,0:T(8,128)} %all-reduce.3.cloned.1.call-done) | copy-start | bytes 983044
  142.3 3.9 %collective-permute-start.2 = (f32[16,512]{1,0:T(8,128)S(1)}, f32[16,512]{1,0:T(8,128)S(1)}, u32[]{:S(2)}, u32[]{:S(2)}) collective-permute-start(f32[16,512]{1,0:T(8,128)S(1)} %convolution_bitcast_fusion), channel_id=1, source_target_pairs={{0,16},{8,24},{16,0},{24,8},{1,17},{9,25},{17,1},{25,9},{2,18},{10... | collective-permute-start | bytes 98312 | tf_op jit(solution)/shard_map/ppermute | solution.py:10
  256.0 7.8 %collective-permute-start.3 = (f32[16,5120]{1,0:T(8,128)}, f32[16,5120]{1,0:T(8,128)S(1)}, u32[]{:S(2)}, u32[]{:S(2)}) collective-permute-start(f32[16,5120]{1,0:T(8,128)} %all-reduce.5.cloned.1.call-done), channel_id=1, source_target_pairs={{0,16},{8,24},{16,0},{24,8},{1,17},{9,25},{17,1},{25,9},{2,18},{10... | collective-permute-start | bytes 983048 | tf_op jit(solution)/shard_map/ppermute | solution.py:10
Sparse Core Ops, SparseCore 0:
  53.5 72.2 all-reduce.2
  185.4 70.5 all-reduce.4
